TPU v7x, 32 devices: a whole 2x2x4 slice. The times are simulated.
32 devices in a mesh: cp: 4 (over y, x), grp: 8 (over z, core).
Axes of the slice: x: 2, y: 2, z: 4, core: 2. Of those that a mesh axis runs over, the one named last changes fastest.
Arguments:
- queries: bfloat16 [16, 512, 2048], P('grp', 'cp'), may hold values from -108 to 108
- keys: bfloat16 [16, 512, 2048], P('grp', 'cp'), may hold values from -4 to 4
- values: bfloat16 [16, 512, 2048], P('grp', 'cp'), may hold values from -6 to 6
- lengths: int32 [16], P('grp'), may hold values from 128 to 512
- frame_map: bfloat16 [2048, 2176], replicated, may hold values from -0.125 to 0.125
- proj_weight: bfloat16 [2176, 4096], P('grp', 'cp'), may hold values from -0.125 to 0.125
- head_weight: bfloat16 [4096, 256], P('cp'), may hold values from -0.375 to 0.375
- act_embed: float32 [7, 4096], P(None, 'cp'), may hold values from -0.5 to 0.5
- actions: int32 [16, 7], P('grp'), may hold values from 0 to 255
- action_mask: int32 [16, 7], P('grp'), may hold values 0 or 1
- group_ids: int32 [16], P('grp'), may hold values from 0 to 1
- rewards: float32 [16], P('grp'), may hold values from -6 to 6
Outputs:
- logprobs: float32 [16, 7], P('grp')
- grad_proj: bfloat16 [2176, 4096], P('grp', 'cp')
- grad_head: bfloat16 [4096, 256], P('cp')
All inputs are finite; a program needn't handle non-finite values. No bound on the sum of `action_mask` on one device may be relied on, other than what follows from the above.
Results may differ from a plain program's by a relative error of at most 0.018.
Values may be sent and summed in bfloat16 or wider, within the bound.
A program may use at most 128 MiB of HBM per device.

v0:
```python
import math
import jax
import jax.numpy as jnp
from jax import lax
from jax.sharding import PartitionSpec as P

HD = 128
SQRT_HALF = 0.7071067811865476
INV_ROOT_TAU = 0.3989422804014327
NEG_LARGE = -1e30


def gelu_exact(values_in):
    return 0.5 * values_in * (1.0 + lax.erf(values_in * SQRT_HALF))


def gelu_slope(values_in):
    return (
        0.5 * (1.0 + lax.erf(values_in * SQRT_HALF))
        + values_in * jnp.exp(-0.5 * values_in * values_in) * INV_ROOT_TAU
    )


def fetch_columns(proj_weight):
    return lax.all_gather(proj_weight, "grp", axis=0, tiled=True)


def attention(queries, keys, values, lengths):
    episodes_here, tokens_here, att_width = queries.shape
    head_count = att_width // HD
    query_heads = queries.reshape(episodes_here, tokens_here, head_count, HD)
    key_heads = keys.reshape(episodes_here, tokens_here, head_count, HD)
    value_heads = values.reshape(episodes_here, tokens_here, head_count, HD)
    query_all, key_all, value_all = (
        lax.all_to_all(query_heads, "cp", split_axis=2, concat_axis=1, tiled=True),
        lax.all_to_all(key_heads, "cp", split_axis=2, concat_axis=1, tiled=True),
        lax.all_to_all(value_heads, "cp", split_axis=2, concat_axis=1, tiled=True),
    )
    seq_span = query_all.shape[1]
    scores = jnp.einsum(
        "eihd,ejhd->ehij", query_all, key_all, preferred_element_type=jnp.float32
    ) / math.sqrt(HD)
    live_keys = (jnp.arange(seq_span, dtype=jnp.int32)[None, :] < lengths[:, None])[
        :, None, None, :
    ]
    scores = jnp.where(live_keys, scores, NEG_LARGE)
    row_max = jnp.max(scores, axis=-1, keepdims=True)
    probs = jnp.where(live_keys, jnp.exp(scores - row_max), 0.0)
    row_total = jnp.sum(probs, axis=-1)
    weighted = jnp.einsum(
        "ehij,ejhd->eihd", probs.astype(jnp.bfloat16), value_all, preferred_element_type=jnp.float32
    )
    output = (weighted / jnp.transpose(row_total, (0, 2, 1))[..., None]).astype(jnp.bfloat16)
    returned = lax.all_to_all(output, "cp", split_axis=1, concat_axis=2, tiled=True)
    return returned.reshape(episodes_here, tokens_here, att_width)


def per_device(
    queries,
    keys,
    values,
    lengths,
    frame_map,
    proj_weight,
    head_weight,
    act_embed,
    actions,
    action_mask,
    group_ids,
    rewards,
):
    episodes_here, tokens_here, att_width = queries.shape
    action_count = act_embed.shape[0]
    lengths_real = lengths.astype(jnp.float32)
    attended = attention(queries, keys, values, lengths)
    proj_cols = fetch_columns(proj_weight)
    frames = jnp.dot(
        attended.reshape(episodes_here * tokens_here, att_width),
        frame_map,
        preferred_element_type=jnp.float32,
    )
    frames = frames.astype(jnp.bfloat16).reshape(episodes_here, tokens_here, frame_map.shape[1])
    all_frames = lax.all_gather(frames, "cp", axis=1, tiled=True)
    seq_span = all_frames.shape[1]
    flat_frames = all_frames.reshape(episodes_here * seq_span, all_frames.shape[2])
    col_count = proj_cols.shape[1]
    pre_act = jnp.dot(flat_frames, proj_cols, preferred_element_type=jnp.float32).reshape(
        episodes_here, seq_span, col_count
    )
    hidden = gelu_exact(pre_act)
    token_mask = (jnp.arange(seq_span, dtype=jnp.int32)[None, :] < lengths[:, None]).astype(
        jnp.float32
    )
    pooled = jnp.sum(token_mask[:, :, None] * hidden, axis=1) / lengths_real[:, None]
    sum_input = pooled[:, None, :] + act_embed[None, :, :]
    head_input = sum_input.astype(jnp.bfloat16).reshape(episodes_here * action_count, col_count)
    partial_logits = jnp.dot(head_input, head_weight, preferred_element_type=jnp.float32)
    episodes_total = episodes_here * lax.axis_size("grp")
    group_count = max(1, episodes_total // 8)
    membership = (group_ids[:, None] == jnp.arange(group_count, dtype=jnp.int32)[None, :]).astype(
        jnp.float32
    )
    masked = action_mask.astype(jnp.float32)
    logits = lax.psum(partial_logits, "cp")
    reward_sums, squares, group_sizes, mask_total = lax.psum(
        (
            jnp.sum(membership * rewards[:, None], axis=0),
            jnp.sum(membership * (rewards * rewards)[:, None], axis=0),
            jnp.sum(membership, axis=0),
            jnp.sum(masked),
        ),
        "grp",
    )
    log_all = jax.nn.log_softmax(logits, axis=-1)
    bin_ids = jnp.arange(head_weight.shape[1], dtype=jnp.int32)
    picked = (actions.reshape(-1)[:, None] == bin_ids[None, :]).astype(jnp.float32)
    logprobs = jnp.sum(picked * log_all, axis=-1).reshape(episodes_here, action_count)
    size_floor = jnp.maximum(group_sizes, 1.0)
    group_mean = reward_sums / size_floor
    variance = squares / size_floor - group_mean * group_mean
    group_scale = jnp.sqrt(jnp.maximum(variance, 1.0))
    advantage = (rewards - jnp.sum(membership * group_mean[None, :], axis=1)) / jnp.sum(
        membership * group_scale[None, :], axis=1
    )
    loss_weight = (-masked * advantage[:, None] / jnp.maximum(mask_total, 1.0)).reshape(-1)
    logit_grad = (loss_weight[:, None] * (picked - jnp.exp(log_all))).astype(jnp.bfloat16)
    head_term = lax.dot_general(
        head_input, logit_grad, (((0,), (0,)), ((), ())), preferred_element_type=jnp.float32
    )
    grad_head = lax.psum(head_term.astype(jnp.bfloat16), "grp")
    pull_back = lax.dot_general(
        logit_grad, head_weight, (((1,), (1,)), ((), ())), preferred_element_type=jnp.float32
    )
    pool_grad = jnp.sum(pull_back.reshape(episodes_here, action_count, col_count), axis=1)
    scaled_mask = token_mask / lengths_real[:, None]
    act_grad = (scaled_mask[:, :, None] * pool_grad[:, None, :] * gelu_slope(pre_act)).astype(
        jnp.bfloat16
    )
    act_flat = act_grad.reshape(episodes_here * seq_span, col_count)
    grad_proj = lax.psum_scatter(
        lax.dot_general(
            flat_frames, act_flat, (((0,), (0,)), ((), ())), preferred_element_type=jnp.float32
        ).astype(jnp.bfloat16),
        "grp",
        scatter_dimension=0,
        tiled=True,
    )
    return (logprobs, grad_proj, grad_head)


def solution(mesh):
    in_specs = (
        P("grp", "cp", None),
        P("grp", "cp", None),
        P("grp", "cp", None),
        P("grp"),
        P(),
        P("grp", "cp"),
        P("cp", None),
        P(None, "cp"),
        P("grp", None),
        P("grp", None),
        P("grp"),
        P("grp"),
    )
    out_specs = (P("grp", None), P("grp", "cp"), P("cp", None))
    return jax.shard_map(
        per_device, mesh=mesh, in_specs=in_specs, out_specs=out_specs, check_vma=False
    )
```

profile of v0, /device:TPU:0, one launch (start us, length us, event | category | flops | bytes accessed | tf_op | source)
XLA Modules:
  0.0 302.5 jit_solution(11430559681268954911)
XLA Ops:
  7.2 0.0 copy-start
  7.2 0.0 all-gather.5.cloned.1.call-start
  7.2 0.7 all-gather.5.cloned.1.call-update
  7.9 1.6 copy.51
  9.5 1.0 copy.52
  10.6 5.2 %all-to-all-start = ((bf16[2,128,16,128]{1,3,0,2:T(8,128)(2,1)}), bf16[2,128,16,128]{1,3,0,2:T(8,128)(2,1)S(1)}, u32[]{:S(2)}, u32[]{:S(2)}) async-start(bf16[2,128,16,128]{1,3,0,2:T(8,128)(2,1)} %copy.52), calls=%async_computation | async-start | bytes 2097152 | tf_op jit(solution)/shard_map/all_to_all | solution.py:35
  15.8 1.6 copy.55
  17.4 1.1 copy.56
  18.5 10.9 %all-to-all-done = bf16[2,128,16,128]{1,3,0,2:T(8,128)(2,1)S(1)} async-done(((bf16[2,128,16,128]{1,3,0,2:T(8,128)(2,1)}), bf16[2,128,16,128]{1,3,0,2:T(8,128)(2,1)S(1)}, u32[]{:S(2)}, u32[]{:S(2)}) %all-to-all-start) | async-done | bytes 1048608 | tf_op jit(solution)/shard_map/all_to_all | solution.py:35
  29.4 3.5 %all-to-all-start.1 = ((bf16[2,128,16,128]{1,3,0,2:T(8,128)(2,1)}), bf16[2,128,16,128]{1,3,0,2:T(8,128)(2,1)S(1)}, u32[]{:S(2)}, u32[]{:S(2)}) async-start(bf16[2,128,16,128]{1,3,0,2:T(8,128)(2,1)} %copy.56), calls=%async_computation.1 | async-start | bytes 2097152 | tf_op jit(solution)/shard_map/all_to_all | solution.py:36
  32.9 2.3 copy.59
  35.2 2.3 copy.60
  37.5 8.6 %all-to-all-done.1 = bf16[2,128,16,128]{1,3,0,2:T(8,128)(2,1)S(1)} async-done(((bf16[2,128,16,128]{1,3,0,2:T(8,128)(2,1)}), bf16[2,128,16,128]{1,3,0,2:T(8,128)(2,1)S(1)}, u32[]{:S(2)}, u32[]{:S(2)}) %all-to-all-start.1) | async-done | bytes 1048608 | tf_op jit(solution)/shard_map/all_to_all | solution.py:36
  46.2 4.3 %all-to-all-start.2 = ((bf16[2,128,16,128]{1,3,0,2:T(8,128)(2,1)}), bf16[2,128,16,128]{1,3,0,2:T(8,128)(2,1)}, u32[]{:S(2)}, u32[]{:S(2)}) async-start(bf16[2,128,16,128]{1,3,0,2:T(8,128)(2,1)} %copy.60), calls=%async_computation.2 | async-start | bytes 2097152 | tf_op jit(solution)/shard_map/all_to_all | solution.py:37
  50.4 0.0 all-gather.3.cloned.1.call-start
  50.5 0.0 copy-done.5
  50.5 0.1 fusion.31
  50.6 1.3 copy.54
  51.9 1.4 copy.58
  53.2 10.5 %all-to-all-done.2 = bf16[2,128,16,128]{1,3,0,2:T(8,128)(2,1)} async-done(((bf16[2,128,16,128]{1,3,0,2:T(8,128)(2,1)}), bf16[2,128,16,128]{1,3,0,2:T(8,128)(2,1)}, u32[]{:S(2)}, u32[]{:S(2)}) %all-to-all-start.2) | async-done | bytes 1048608 | tf_op jit(solution)/shard_map/all_to_all | solution.py:37
  63.7 1.6 copy.62
  65.4 0.0 copy-done.1
  65.4 6.8 %fusion.33 = (f32[2,4,512]{2,1,0:T(4,128)S(1)}, bf16[2,4,512,512]{2,3,1,0:T(8,128)(2,1)}) fusion(pred[2,512]{1,0:T(4,128)(4,1)S(1)} %get-tuple-element.15, bf16[2,512,4,128]{3,1,2,0:T(8,128)(2,1)S(1)} %bitcast.54, bf16[2,512,4,128]{3,1,2,0:T(8,128)(2,1)} %bitcast.55), kind=kOutput, calls=%fused_computation.58 | convolution fusion | flops 549454336 | bytes 6308864 | tf_op jit(solution)/shard_map/sub | solution.py:48
  72.2 3.9 %fusion.16 = bf16[2,512,4,128]{3,1,2,0:T(8,128)(2,1)S(1)} fusion(bf16[2,512,4,128]{3,1,2,0:T(8,128)(2,1)S(1)} %bitcast.56, bf16[2,4,512,512]{2,3,1,0:T(8,128)(2,1)} %get-tuple-element.17, f32[2,512,4]{1,2,0:T(4,128)S(1)} %bitcast.57), kind=kOutput, calls=%fused_computation.23 | convolution fusion | flops 537919488 | bytes 6307840 | tf_op jit(solution)/shard_map/ehij,ejhd->eihd/dot_general | solution.py:50
  76.1 0.8 copy.64
  76.9 16.1 %all_to_all.69 = bf16[2,512,4,128]{3,2,0,1:T(4,128)(2,1)S(1)} all-to-all(bf16[2,512,4,128]{3,2,0,1:T(4,128)(2,1)S(1)} %copy.64), channel_id=1, replica_groups=mesh['cp'=4,'grp'=8] {'cp'}, dimensions={1} | all-to-all | bytes 2097152 | tf_op jit(solution)/shard_map/all_to_all | solution.py:54
  93.0 0.4 copy.73
  93.4 0.8 reshape_reshape.3
  94.2 0.0 copy-start.4
  94.2 0.0 copy-start.6
  94.2 0.0 copy-start.3
  94.3 0.0 copy-start.7
  94.3 7.2 %convolution_convert_fusion = bf16[256,2176]{1,0:T(8,128)(2,1)} fusion(bf16[256,2048]{1,0:T(8,128)(2,1)S(1)} %reshape_reshape.3, bf16[2048,2176]{1,0:T(8,128)(2,1)} %param.16), kind=kOutput, calls=%fused_computation.21 | convolution fusion | flops 2282258432 | bytes 11075584 | tf_op jit(solution)/shard_map/dot_general | solution.py:77
  101.5 0.0 all-gather.3.cloned.1.call-update
  101.5 0.0 all-reduce.3.cloned.1.call-start
  101.6 0.0 copy-done.4
  101.6 0.0 copy-done.6
  101.6 0.6 convert_reduce_fusion.1
  102.2 0.1 select_reduce_fusion.2
  102.3 15.2 %all-reduce = (f32[]{:T(128)}, f32[2]{0:T(128)S(1)}, f32[2]{0:T(128)S(1)}, f32[2]{0:T(128)S(1)}) all-reduce(f32[]{:T(128)} %convert_reduce_fusion.1, f32[2]{0:T(128)S(1)} %get-tuple-element.7, f32[2]{0:T(128)S(1)} %get-tuple-element.6, f32[2]{0:T(128)S(1)} %get-tuple-element.5), channel_id=1, replica_groups=mesh['cp'=4,'grp'=8] {'grp'}, use_global_device_ids=true, to_apply=%region_16.17 | all-reduce | flops 7 | bytes 56 | tf_op jit(solution)/shard_map/psum | solution.py:105
  117.5 0.0 copy-done.7
  117.5 0.1 eq.28
  118.3 0.2 select_reduce_fusion.3
  118.5 0.1 multiply_divide_fusion
  118.5 0.1 mul.133
  118.6 0.1 broadcast_divide_fusion.1
  118.7 37.5 %all-gather.3.cloned.1.call-done = bf16[2,512,2176]{2,1,0:T(8,128)(2,1)} async-done(((bf16[2,128,2176]{2,1,0:T(8,128)(2,1)}), bf16[2,512,2176]{2,1,0:T(8,128)(2,1)}) %all-gather.3.cloned.1.call-update) | async-done | bytes 4456464 | tf_op jit(solution)/shard_map/all_gather | solution.py:83
  156.2 9.9 %multiply_reduce_fusion = (f32[2,1024]{1,0:T(2,128)S(1)}, f32[2,512,1024]{2,1,0:T(8,128)}) fusion(f32[2,512]{1,0:T(2,128)S(1)} %get-tuple-element.14, bf16[2,512,2176]{2,1,0:T(8,128)(2,1)} %all-gather.3.cloned.1.call-done, bf16[2176,1024]{1,0:T(8,128)(2,1)} %all-gather.5.cloned.1.call-done), kind=kOutput, calls=%fused_computation.14 | convolution fusion | flops 4569692160 | bytes 13119488 | tf_op jit(solution)/shard_map/dot_general | solution.py:87
  166.1 0.1 broadcast_divide_fusion
  166.2 0.2 fusion.34
  166.4 15.1 %psum.42 = f32[14,256]{1,0:T(8,128)S(1)} all-reduce(f32[14,256]{1,0:T(8,128)S(1)} %fusion.34), channel_id=1, replica_groups=mesh['cp'=4,'grp'=8] {'cp'}, use_global_device_ids=true, to_apply=%region_3.4 | all-reduce | flops 3584 | bytes 28672 | tf_op jit(solution)/shard_map/psum | solution.py:104
  181.5 0.1 reduce_max.20
  181.6 0.2 exponential_reduce_fusion
  181.8 0.3 fusion.32
  182.1 1.2 convolution_convert_fusion.1
  183.3 0.0 all-reduce.3.cloned.1.call-update
  183.3 0.0 reduce-scatter.2.cloned.1.call-start
  183.4 10.3 %bitcast_convert_fusion = bf16[2176,1024]{1,0:T(8,128)(2,1)} fusion(bf16[2,512,2176]{2,1,0:T(8,128)(2,1)} %all-gather.3.cloned.1.call-done, f32[2,512,1024]{2,1,0:T(8,128)} %get-tuple-element.19, f32[2,1024]{1,0:T(2,128)S(1)} %reduce_sum.110, f32[2,512]{1,0:T(2,128)S(1)} %broadcast_divide_fusion.1), kind=kOutput, calls=%fused_computation.1 | convolution fusion | flops 4577165312 | bytes 13119488 | tf_op jit(solution)/shard_map/dot_general | solution.py:141
  193.7 0.0 reduce-scatter.2.cloned.1.call-update
  193.7 0.2 select_reduce_fusion
  193.9 0.6 reshape.138
  194.5 45.4 %all-reduce.3.cloned.1.call-done = bf16[1024,256]{1,0:T(8,128)(2,1)} async-done(((bf16[1024,256]{1,0:T(8,128)(2,1)}), bf16[1024,256]{1,0:T(8,128)(2,1)}) %all-reduce.3.cloned.1.call-update) | async-done | bytes 524304 | tf_op jit(solution)/shard_map/psum | solution.py:130
  239.9 54.2 %reduce-scatter.2.cloned.1.call-done = bf16[272,1024]{1,0:T(8,128)(2,1)} async-done(((bf16[2176,1024]{1,0:T(8,128)(2,1)}), bf16[272,1024]{1,0:T(8,128)(2,1)}) %reduce-scatter.2.cloned.1.call-update) | async-done | bytes 557072 | tf_op jit(solution)/shard_map/reduce_scatter | solution.py:140
  294.1 1.9 copy.75
  (16 shorter events, 0.1 us)
Async XLA Ops:
  7.2 159.1 %copy-start = (bf16[1024,256]{1,0:T(8,128)(2,1)S(1)}, bf16[1024,256]{1,0:T(8,128)(2,1)}, u32[]{:S(2)}) copy-start(bf16[1024,256]{1,0:T(8,128)(2,1)} %param.18) | copy-start | bytes 1572868
  7.2 111.5 %all-gather.5.cloned.1.call-start = ((), (), s32[]{:S(2)}) async-start(), calls=%async_computation.6 | async-start | bytes 5013504 | tf_op jit(solution)/shard_map/all_gather | solution.py:25
  10.6 18.8 %all-to-all-start = ((bf16[2,128,16,128]{1,3,0,2:T(8,128)(2,1)}), bf16[2,128,16,128]{1,3,0,2:T(8,128)(2,1)S(1)}, u32[]{:S(2)}, u32[]{:S(2)}) async-start(bf16[2,128,16,128]{1,3,0,2:T(8,128)(2,1)} %copy.52), calls=%async_computation | async-start | bytes 2097152 | tf_op jit(solution)/shard_map/all_to_all | solution.py:35
  18.5 32.0 %copy-start.5 = (s32[2]{0:T(128)S(1)}, s32[2]{0:T(128)}, u32[]{:S(2)}) copy-start(s32[2]{0:T(128)} %param.15) | copy-start | bytes 28
  29.4 16.8 %all-to-all-start.1 = ((bf16[2,128,16,128]{1,3,0,2:T(8,128)(2,1)}), bf16[2,128,16,128]{1,3,0,2:T(8,128)(2,1)S(1)}, u32[]{:S(2)}, u32[]{:S(2)}) async-start(bf16[2,128,16,128]{1,3,0,2:T(8,128)(2,1)} %copy.56), calls=%async_computation.1 | async-start | bytes 2097152 | tf_op jit(solution)/shard_map/all_to_all | solution.py:36
  46.2 17.6 %all-to-all-start.2 = ((bf16[2,128,16,128]{1,3,0,2:T(8,128)(2,1)}), bf16[2,128,16,128]{1,3,0,2:T(8,128)(2,1)}, u32[]{:S(2)}, u32[]{:S(2)}) async-start(bf16[2,128,16,128]{1,3,0,2:T(8,128)(2,1)} %copy.60), calls=%async_computation.2 | async-start | bytes 2097152 | tf_op jit(solution)/shard_map/all_to_all | solution.py:37
  50.4 105.8 %all-gather.3.cloned.1.call-start = ((), (), s32[]{:S(2)}) async-start(), calls=%async_computation.5 | async-start | bytes 5570560 | tf_op jit(solution)/shard_map/all_gather | solution.py:83
  51.9 13.5 %copy-start.1 = (bf16[2,4,128,4,128]{4,2,1,3,0:T(8,128)(2,1)S(1)}, bf16[2,4,128,4,128]{4,2,1,3,0:T(8,128)(2,1)}, u32[]{:S(2)}) copy-start(bf16[2,4,128,4,128]{4,2,1,3,0:T(8,128)(2,1)} %copy.54) | copy-start | bytes 3145732
  94.2 7.3 %copy-start.4 = (f32[2]{0:T(128)S(1)}, f32[2]{0:T(128)}, u32[]{:S(2)}) copy-start(f32[2]{0:T(128)} %param.23) | copy-start | bytes 28
  94.2 7.4 %copy-start.6 = (s32[2,7]{1,0:T(2,128)S(1)}, s32[2,7]{1,0:T(2,128)}, u32[]{:S(2)}) copy-start(s32[2,7]{1,0:T(2,128)} %param.21) | copy-start | bytes 172
  94.2 8.0 %copy-start.3 = (s32[2]{0:T(128)S(1)}, s32[2]{0:T(128)}, u32[]{:S(2)}) copy-start(s32[2]{0:T(128)} %param.22) | copy-start | bytes 28
  94.3 23.3 %copy-start.7 = (s32[2,7]{1,0:T(2,128)S(1)}, s32[2,7]{1,0:T(2,128)}, u32[]{:S(2)}) copy-start(s32[2,7]{1,0:T(2,128)} %param.20) | copy-start | bytes 172
  101.5 138.4 %all-reduce.3.cloned.1.call-start = ((), (), s32[]{:S(2)}) async-start(), calls=%async_computation.8 | async-start | bytes 1048576 | tf_op jit(solution)/shard_map/psum | solution.py:130
  156.2 10.0 %copy-start.2 = (f32[7,1024]{1,0:T(8,128)S(1)}, f32[7,1024]{1,0:T(8,128)}, u32[]{:S(2)}) copy-start(f32[7,1024]{1,0:T(8,128)} %param.19) | copy-start | bytes 86020
  183.3 110.8 %reduce-scatter.2.cloned.1.call-start = ((), (), s32[]{:S(2)}) async-start(), calls=%async_computation.7 | async-start | bytes 5013504 | tf_op jit(solution)/shard_map/reduce_scatter | solution.py:140
Sparse Core Ops, SparseCore 0:
  9.6 51.7 all-gather.4
  101.6 54.4 all-gather.2
  183.4 56.4 all-reduce.2
  242.7 51.4 reduce-scatter.1
where the time goes:
time: 303 us
  waiting for transfers between devices  168 us (55%)
  blocking collectives  46.4 us (15%)
  matrix products  39.8 us (13%)
  local copies, waits for them, and re-layouts  19 us (6%)
  between operations  14.6 us (5%)
  starting transfers between devices  13.1 us (4%)
    reduce_scatter x1, waiting for transfers between devices, per_device(): lax.psum_scatter(lax.dot_general(flat_frames, act_flat, (((0,), (0,)), ((...  54.2 us
    psum x1, waiting for transfers between devices, per_device(): grad_head = lax.psum(head_term.astype(jnp.bfloat16), 'grp')  45.4 us
    all_gather x1, waiting for transfers between devices, per_device(): all_frames = lax.all_gather(frames, 'cp', axis=1, tiled=True)  37.5 us
    all_to_all x1, blocking collectives, attention(): lax.all_to_all(output, 'cp', split_axis=1, concat_axis=2, tiled=True)  16.1 us
    psum x1, blocking collectives, per_device(): lax.psum((jnp.sum(membership * rewards[:, None], axis=0), jnp.sum(members...  15.2 us
    psum x1, blocking collectives, per_device(): logits = lax.psum(partial_logits, 'cp')  15.1 us
    all_to_all x1, waiting for transfers between devices, attention(): lax.all_to_all(query_heads, 'cp', split_axis=2, concat_axis=1, tiled=True)  10.9 us
    all_to_all x1, waiting for transfers between devices, attention(): lax.all_to_all(value_heads, 'cp', split_axis=2, concat_axis=1, tiled=True)  10.5 us
  transfers between devices with their start and end apart: 7, of which 6 were waited for; matrix products, arithmetic and copies ran while one was open for 15% of the time, Pallas kernels for 0%

commit v1 on v0

--- a/solution.py
+++ b/solution.py
@@ -127,7 +127,9 @@
     head_term = lax.dot_general(
         head_input, logit_grad, (((0,), (0,)), ((), ())), preferred_element_type=jnp.float32
     )
-    grad_head = lax.psum(head_term.astype(jnp.bfloat16), "grp")
+    part = head_term.astype(jnp.bfloat16)
+    pieces = lax.all_gather(part, "grp")
+    grad_head = jnp.sum(pieces, axis=0)
     pull_back = lax.dot_general(
         logit_grad, head_weight, (((1,), (1,)), ((), ())), preferred_element_type=jnp.float32
     )

time: 303 us -> 291 us (0.960)
  waiting for transfers between devices: 168 us -> 154 us
  other arithmetic: 1.73 us -> 5.43 us
    psum x1 -> x0, waiting for transfers between devices: 45.4 us -> none  [per_device(): grad_head = lax.psum(head_term.astype(jnp.bfloat16), 'grp')]
    all_gather x0 -> x1, waiting for transfers between devices: none -> 35.4 us  [per_device(): pieces = lax.all_gather(part, 'grp')]
    reduce_scatter x1, waiting for transfers between devices: 54.2 us -> 50.3 us  [per_device(): lax.psum_scatter(lax.dot_general(flat_frames, act_flat, (((0,), (0,)), ((...]
    reduce_sum x0 -> x1, other arithmetic: none -> 3.7 us  [per_device(): grad_head = jnp.sum(pieces, axis=0)]
    unnamed x20 -> x19, local copies, waits for them, and re-layouts: 7.4 us -> 5.53 us
  transfers between devices with their start and end apart: 7 -> 7, of which waited for: 6 -> 6; matrix products, arithmetic and copies ran while one was open for 15% -> 17% of each run, Pallas kernels for 0% -> 0%
where the time goes in v1:
time: 291 us
  waiting for transfers between devices  154 us (53%)
  blocking collectives  46.4 us (16%)
  matrix products  39.7 us (14%)
  local copies, waits for them, and re-layouts  17.1 us (6%)
  between operations  14.6 us (5%)
  starting transfers between devices  13.1 us (5%)
  other arithmetic  5.43 us (2%)
    reduce_scatter x1, waiting for transfers between devices, per_device(): lax.psum_scatter(lax.dot_general(flat_frames, act_flat, (((0,), (0,)), ((...  50.3 us
    all_gather x1, waiting for transfers between devices, per_device(): all_frames = lax.all_gather(frames, 'cp', axis=1, tiled=True)  37.6 us
    all_gather x1, waiting for transfers between devices, per_device(): pieces = lax.all_gather(part, 'grp')  35.4 us
    all_to_all x1, blocking collectives, attention(): lax.all_to_all(output, 'cp', split_axis=1, concat_axis=2, tiled=True)  16.1 us
    psum x1, blocking collectives, per_device(): lax.psum((jnp.sum(membership * rewards[:, None], axis=0), jnp.sum(members...  15.2 us
    psum x1, blocking collectives, per_device(): logits = lax.psum(partial_logits, 'cp')  15.1 us
    all_to_all x1, waiting for transfers between devices, attention(): lax.all_to_all(query_heads, 'cp', split_axis=2, concat_axis=1, tiled=True)  10.9 us
    all_to_all x1, waiting for transfers between devices, attention(): lax.all_to_all(value_heads, 'cp', split_axis=2, concat_axis=1, tiled=True)  10.5 us
  transfers between devices with their start and end apart: 7, of which 6 were waited for; matrix products, arithmetic and copies ran while one was open for 17% of the time, Pallas kernels for 0%

profile of v1, /device:TPU:0, one launch (start us, length us, event | category | flops | bytes accessed | tf_op | source)
XLA Modules:
  0.0 290.5 jit_solution(16228729840222325299)
XLA Ops:
  7.2 0.0 copy-start
  7.2 0.0 all-gather.7.cloned.1.call-start
  7.2 0.7 all-gather.7.cloned.1.call-update
  7.9 1.6 copy.51
  9.5 1.0 copy.52
  10.6 5.2 %all-to-all-start = ((bf16[2,128,16,128]{1,3,0,2:T(8,128)(2,1)}), bf16[2,128,16,128]{1,3,0,2:T(8,128)(2,1)S(1)}, u32[]{:S(2)}, u32[]{:S(2)}) async-start(bf16[2,128,16,128]{1,3,0,2:T(8,128)(2,1)} %copy.52), calls=%async_computation | async-start | bytes 2097152 | tf_op jit(solution)/shard_map/all_to_all | solution.py:35
  15.8 1.6 copy.55
  17.4 1.1 copy.56
  18.5 10.9 %all-to-all-done = bf16[2,128,16,128]{1,3,0,2:T(8,128)(2,1)S(1)} async-done(((bf16[2,128,16,128]{1,3,0,2:T(8,128)(2,1)}), bf16[2,128,16,128]{1,3,0,2:T(8,128)(2,1)S(1)}, u32[]{:S(2)}, u32[]{:S(2)}) %all-to-all-start) | async-done | bytes 1048608 | tf_op jit(solution)/shard_map/all_to_all | solution.py:35
  29.4 3.5 %all-to-all-start.1 = ((bf16[2,128,16,128]{1,3,0,2:T(8,128)(2,1)}), bf16[2,128,16,128]{1,3,0,2:T(8,128)(2,1)S(1)}, u32[]{:S(2)}, u32[]{:S(2)}) async-start(bf16[2,128,16,128]{1,3,0,2:T(8,128)(2,1)} %copy.56), calls=%async_computation.1 | async-start | bytes 2097152 | tf_op jit(solution)/shard_map/all_to_all | solution.py:36
  32.9 2.3 copy.59
  35.2 2.3 copy.60
  37.5 8.6 %all-to-all-done.1 = bf16[2,128,16,128]{1,3,0,2:T(8,128)(2,1)S(1)} async-done(((bf16[2,128,16,128]{1,3,0,2:T(8,128)(2,1)}), bf16[2,128,16,128]{1,3,0,2:T(8,128)(2,1)S(1)}, u32[]{:S(2)}, u32[]{:S(2)}) %all-to-all-start.1) | async-done | bytes 1048608 | tf_op jit(solution)/shard_map/all_to_all | solution.py:36
  46.2 4.3 %all-to-all-start.2 = ((bf16[2,128,16,128]{1,3,0,2:T(8,128)(2,1)}), bf16[2,128,16,128]{1,3,0,2:T(8,128)(2,1)}, u32[]{:S(2)}, u32[]{:S(2)}) async-start(bf16[2,128,16,128]{1,3,0,2:T(8,128)(2,1)} %copy.60), calls=%async_computation.2 | async-start | bytes 2097152 | tf_op jit(solution)/shard_map/all_to_all | solution.py:37
  50.4 0.0 all-gather.5.cloned.1.call-start
  50.5 0.0 copy-done.5
  50.5 0.1 fusion.31
  50.6 1.3 copy.54
  51.9 1.4 copy.58
  53.2 10.5 %all-to-all-done.2 = bf16[2,128,16,128]{1,3,0,2:T(8,128)(2,1)} async-done(((bf16[2,128,16,128]{1,3,0,2:T(8,128)(2,1)}), bf16[2,128,16,128]{1,3,0,2:T(8,128)(2,1)}, u32[]{:S(2)}, u32[]{:S(2)}) %all-to-all-start.2) | async-done | bytes 1048608 | tf_op jit(solution)/shard_map/all_to_all | solution.py:37
  63.7 1.6 copy.62
  65.4 0.0 copy-done.1
  65.4 6.8 %fusion.33 = (f32[2,4,512]{2,1,0:T(4,128)S(1)}, bf16[2,4,512,512]{2,3,1,0:T(8,128)(2,1)}) fusion(pred[2,512]{1,0:T(4,128)(4,1)S(1)} %get-tuple-element.15, bf16[2,512,4,128]{3,1,2,0:T(8,128)(2,1)S(1)} %bitcast.56, bf16[2,512,4,128]{3,1,2,0:T(8,128)(2,1)} %bitcast.57), kind=kOutput, calls=%fused_computation.58 | convolution fusion | flops 549454336 | bytes 6308864 | tf_op jit(solution)/shard_map/sub | solution.py:48
  72.2 3.9 %fusion.16 = bf16[2,512,4,128]{3,1,2,0:T(8,128)(2,1)S(1)} fusion(bf16[2,512,4,128]{3,1,2,0:T(8,128)(2,1)S(1)} %bitcast.58, bf16[2,4,512,512]{2,3,1,0:T(8,128)(2,1)} %get-tuple-element.17, f32[2,512,4]{1,2,0:T(4,128)S(1)} %bitcast.59), kind=kOutput, calls=%fused_computation.23 | convolution fusion | flops 537919488 | bytes 6307840 | tf_op jit(solution)/shard_map/ehij,ejhd->eihd/dot_general | solution.py:50
  76.1 0.8 copy.64
  76.9 16.1 %all_to_all.69 = bf16[2,512,4,128]{3,2,0,1:T(4,128)(2,1)S(1)} all-to-all(bf16[2,512,4,128]{3,2,0,1:T(4,128)(2,1)S(1)} %copy.64), channel_id=1, replica_groups=mesh['cp'=4,'grp'=8] {'cp'}, dimensions={1} | all-to-all | bytes 2097152 | tf_op jit(solution)/shard_map/all_to_all | solution.py:54
  93.0 0.4 copy.73
  93.4 0.8 reshape_reshape.3
  94.2 0.0 copy-start.4
  94.2 0.0 copy-start.6
  94.2 0.0 copy-start.3
  94.3 0.0 copy-start.7
  94.3 7.2 %convolution_convert_fusion = bf16[256,2176]{1,0:T(8,128)(2,1)} fusion(bf16[256,2048]{1,0:T(8,128)(2,1)S(1)} %reshape_reshape.3, bf16[2048,2176]{1,0:T(8,128)(2,1)} %param.16), kind=kOutput, calls=%fused_computation.21 | convolution fusion | flops 2282258432 | bytes 11075584 | tf_op jit(solution)/shard_map/dot_general | solution.py:77
  101.5 0.0 all-gather.5.cloned.1.call-update
  101.5 0.0 all-gather.9.cloned.1.call-start
  101.6 0.0 copy-done.4
  101.6 0.0 copy-done.6
  101.6 0.6 convert_reduce_fusion.1
  102.2 0.0 copy-done.3
  102.2 0.1 select_reduce_fusion.2
  102.3 15.2 %all-reduce = (f32[]{:T(128)}, f32[2]{0:T(128)S(1)}, f32[2]{0:T(128)S(1)}, f32[2]{0:T(128)S(1)}) all-reduce(f32[]{:T(128)} %convert_reduce_fusion.1, f32[2]{0:T(128)S(1)} %get-tuple-element.7, f32[2]{0:T(128)S(1)} %get-tuple-element.6, f32[2]{0:T(128)S(1)} %get-tuple-element.5), channel_id=1, replica_groups=mesh['cp'=4,'grp'=8] {'grp'}, use_global_device_ids=true, to_apply=%region_16.17 | all-reduce | flops 7 | bytes 56 | tf_op jit(solution)/shard_map/psum | solution.py:105
  117.5 0.1 eq.28
  118.3 0.2 select_reduce_fusion.3
  118.5 0.1 multiply_divide_fusion
  118.5 0.1 mul.133
  118.6 37.6 %all-gather.5.cloned.1.call-done = bf16[2,512,2176]{2,1,0:T(8,128)(2,1)} async-done(((bf16[2,128,2176]{2,1,0:T(8,128)(2,1)}), bf16[2,512,2176]{2,1,0:T(8,128)(2,1)}) %all-gather.5.cloned.1.call-update) | async-done | bytes 4456464 | tf_op jit(solution)/shard_map/all_gather | solution.py:83
  156.2 9.9 %multiply_reduce_fusion = (f32[2,1024]{1,0:T(2,128)S(1)}, f32[2,512,1024]{2,1,0:T(8,128)}) fusion(f32[2,512]{1,0:T(2,128)S(1)} %get-tuple-element.14, bf16[2,512,2176]{2,1,0:T(8,128)(2,1)} %all-gather.5.cloned.1.call-done, bf16[2176,1024]{1,0:T(8,128)(2,1)} %all-gather.7.cloned.1.call-done), kind=kOutput, calls=%fused_computation.14 | convolution fusion | flops 4569692160 | bytes 13119488 | tf_op jit(solution)/shard_map/dot_general | solution.py:87
  166.1 0.1 broadcast_divide_fusion
  166.2 0.2 fusion.34
  166.4 15.1 %psum.35 = f32[14,256]{1,0:T(8,128)S(1)} all-reduce(f32[14,256]{1,0:T(8,128)S(1)} %fusion.34), channel_id=1, replica_groups=mesh['cp'=4,'grp'=8] {'cp'}, use_global_device_ids=true, to_apply=%region_3.4 | all-reduce | flops 3584 | bytes 28672 | tf_op jit(solution)/shard_map/psum | solution.py:104
  181.5 0.1 reduce_max.20
  181.6 0.2 exponential_reduce_fusion
  181.8 1.2 convolution_convert_fusion.1
  183.0 0.0 all-gather.9.cloned.1.call-update
  183.0 0.0 reduce-scatter.2.cloned.1.call-start
  183.1 0.1 broadcast_divide_fusion.1
  183.1 0.2 fusion.32
  183.5 10.3 %bitcast_convert_fusion = bf16[2176,1024]{1,0:T(8,128)(2,1)} fusion(bf16[2,512,2176]{2,1,0:T(8,128)(2,1)} %all-gather.5.cloned.1.call-done, f32[2,512,1024]{2,1,0:T(8,128)} %get-tuple-element.19, f32[2,1024]{1,0:T(2,128)S(1)} %reduce_sum.122, f32[2,512]{1,0:T(2,128)S(1)} %broadcast_divide_fusion.1), kind=kOutput, calls=%fused_computation.1 | convolution fusion | flops 4577165312 | bytes 13119488 | tf_op jit(solution)/shard_map/dot_general | solution.py:143
  193.7 0.0 reduce-scatter.2.cloned.1.call-update
  193.8 0.2 select_reduce_fusion
  193.9 0.6 reshape.138
  194.6 35.4 %all-gather.9.cloned.1.call-done = bf16[8192,256]{1,0:T(8,128)(2,1)} async-done(((bf16[1024,256]{1,0:T(8,128)(2,1)}), bf16[8192,256]{1,0:T(8,128)(2,1)}) %all-gather.9.cloned.1.call-update) | async-done | bytes 4194320 | tf_op jit(solution)/shard_map/all_gather | solution.py:131
  230.0 3.7 %reduce_sum.123 = bf16[1024,256]{1,0:T(8,128)(2,1)} reduce(bf16[8,1024,256]{2,1,0:T(8,128)(2,1)} %bitcast.47, bf16[]{:T(256)} %constant.33.clone.1), dimensions={0}, to_apply=%region_19.20 | reduce | flops 1835008 | bytes 4718594 | tf_op jit(solution)/shard_map/reduce_sum | solution.py:132
  233.7 50.3 %reduce-scatter.2.cloned.1.call-done = bf16[272,1024]{1,0:T(8,128)(2,1)} async-done(((bf16[2176,1024]{1,0:T(8,128)(2,1)}), bf16[272,1024]{1,0:T(8,128)(2,1)}) %reduce-scatter.2.cloned.1.call-update) | async-done | bytes 557072 | tf_op jit(solution)/shard_map/reduce_scatter | solution.py:142
  (16 shorter events, 0.1 us)
Async XLA Ops:
  7.2 159.1 %copy-start = (bf16[1024,256]{1,0:T(8,128)(2,1)S(1)}, bf16[1024,256]{1,0:T(8,128)(2,1)}, u32[]{:S(2)}) copy-start(bf16[1024,256]{1,0:T(8,128)(2,1)} %param.18) | copy-start | bytes 1572868
  7.2 111.4 %all-gather.7.cloned.1.call-start = ((), (), s32[]{:S(2)}) async-start(), calls=%async_computation.6 | async-start | bytes 5013504 | tf_op jit(solution)/shard_map/all_gather | solution.py:25
  10.6 18.8 %all-to-all-start = ((bf16[2,128,16,128]{1,3,0,2:T(8,128)(2,1)}), bf16[2,128,16,128]{1,3,0,2:T(8,128)(2,1)S(1)}, u32[]{:S(2)}, u32[]{:S(2)}) async-start(bf16[2,128,16,128]{1,3,0,2:T(8,128)(2,1)} %copy.52), calls=%async_computation | async-start | bytes 2097152 | tf_op jit(solution)/shard_map/all_to_all | solution.py:35
  18.5 32.0 %copy-start.5 = (s32[2]{0:T(128)S(1)}, s32[2]{0:T(128)}, u32[]{:S(2)}) copy-start(s32[2]{0:T(128)} %param.15) | copy-start | bytes 28
  29.4 16.8 %all-to-all-start.1 = ((bf16[2,128,16,128]{1,3,0,2:T(8,128)(2,1)}), bf16[2,128,16,128]{1,3,0,2:T(8,128)(2,1)S(1)}, u32[]{:S(2)}, u32[]{:S(2)}) async-start(bf16[2,128,16,128]{1,3,0,2:T(8,128)(2,1)} %copy.56), calls=%async_computation.1 | async-start | bytes 2097152 | tf_op jit(solution)/shard_map/all_to_all | solution.py:36
  46.2 17.6 %all-to-all-start.2 = ((bf16[2,128,16,128]{1,3,0,2:T(8,128)(2,1)}), bf16[2,128,16,128]{1,3,0,2:T(8,128)(2,1)}, u32[]{:S(2)}, u32[]{:S(2)}) async-start(bf16[2,128,16,128]{1,3,0,2:T(8,128)(2,1)} %copy.60), calls=%async_computation.2 | async-start | bytes 2097152 | tf_op jit(solution)/shard_map/all_to_all | solution.py:37
  50.4 105.8 %all-gather.5.cloned.1.call-start = ((), (), s32[]{:S(2)}) async-start(), calls=%async_computation.5 | async-start | bytes 5570560 | tf_op jit(solution)/shard_map/all_gather | solution.py:83
  51.9 13.5 %copy-start.1 = (bf16[2,4,128,4,128]{4,2,1,3,0:T(8,128)(2,1)S(1)}, bf16[2,4,128,4,128]{4,2,1,3,0:T(8,128)(2,1)}, u32[]{:S(2)}) copy-start(bf16[2,4,128,4,128]{4,2,1,3,0:T(8,128)(2,1)} %copy.54) | copy-start | bytes 3145732
  94.2 7.3 %copy-start.4 = (f32[2]{0:T(128)S(1)}, f32[2]{0:T(128)}, u32[]{:S(2)}) copy-start(f32[2]{0:T(128)} %param.23) | copy-start | bytes 28
  94.2 7.4 %copy-start.6 = (s32[2,7]{1,0:T(2,128)S(1)}, s32[2,7]{1,0:T(2,128)}, u32[]{:S(2)}) copy-start(s32[2,7]{1,0:T(2,128)} %param.21) | copy-start | bytes 172
  94.2 8.0 %copy-start.3 = (s32[2]{0:T(128)S(1)}, s32[2]{0:T(128)}, u32[]{:S(2)}) copy-start(s32[2]{0:T(128)} %param.22) | copy-start | bytes 28
  94.3 23.3 %copy-start.7 = (s32[2,7]{1,0:T(2,128)S(1)}, s32[2,7]{1,0:T(2,128)}, u32[]{:S(2)}) copy-start(s32[2,7]{1,0:T(2,128)} %param.20) | copy-start | bytes 172
  101.5 128.5 %all-gather.9.cloned.1.call-start = ((), (), s32[]{:S(2)}) async-start(), calls=%async_computation.8 | async-start | bytes 4718592 | tf_op jit(solution)/shard_map/all_gather | solution.py:131
  156.2 10.0 %copy-start.2 = (f32[7,1024]{1,0:T(8,128)S(1)}, f32[7,1024]{1,0:T(8,128)}, u32[]{:S(2)}) copy-start(f32[7,1024]{1,0:T(8,128)} %param.19) | copy-start | bytes 86020
  183.0 101.0 %reduce-scatter.2.cloned.1.call-start = ((), (), s32[]{:S(2)}) async-start(), calls=%async_computation.7 | async-start | bytes 5013504 | tf_op jit(solution)/shard_map/reduce_scatter | solution.py:142
Sparse Core Ops, SparseCore 0:
  9.6 51.7 all-gather.6
  101.6 54.4 all-gather.4
  183.1 46.8 all-gather.8
  232.7 51.2 reduce-scatter.1
